TPU v7x, 32 devices: a whole 2x2x4 slice. The times are simulated.
32 devices in a mesh: group: 2 (over y), quad: 2 (over core), rows: 8 (over z, x).
Axes of the slice: x: 2, y: 2, z: 4, core: 2. Of those that a mesh axis runs over, the one named last changes fastest.
Arguments:
- solutions: bfloat16 [32, 20480, 128], P('quad', ('group', 'rows')), parts along dimension 1, may hold values from -24 to 24
- point_of_slot: int32 [64], P(('group', 'quad')), parts along dimension 0, may hold values from 0 to 31, each once
- mass_blocks: bfloat16 [160, 20, 128, 128], P(('group', 'rows')), parts along dimension 0, may hold values from -0.125 to 0.125
- block_cols: int32 [160, 20], P(('group', 'rows')), parts along dimension 0, may hold values from 0 to 79, as said below
- sources: bfloat16 [20480, 64], P(('group', 'rows')), parts along dimension 0, may hold values from -0.0625 to 0.0625
Outputs:
- mass_applied: bfloat16 [8, 20480, 128], P('quad', ('group', 'rows')), parts along dimension 1
- reduced: float32 [16, 64, 128], P(('group', 'quad')), parts along dimension 0
There are 2 independent parts, one for each index of `group`. A program takes and returns all parts, laid end to end along the dimension named above; each array names one. Nothing has to cross between parts.
Inputs may be any that keep to these rules, and one draw needn't show every extreme that they name: `point_of_slot`: each contour point sits in exactly one slot. `block_cols`: slot 0 of block row i holds i; every entry c of block row i has |c - i| <= 10; entries of a block row may repeat.
All inputs are finite; a program needn't handle non-finite values.
Results may differ from a plain program's by a relative error of at most 0.0063.
Values may be sent and summed in bfloat16 or wider, within the bound.
A program may use at most 128 MiB of HBM per device.

v0:
```python
import math
import jax
import jax.numpy as jnp
from jax import lax
from jax.sharding import PartitionSpec as P

MOMENTS = 8


def with_halo(block, sides, width):
    for axis, dim in sides:
        count = lax.axis_size(axis)
        forward = [(i, i + 1) for i in range(count - 1)]
        backward = [(target, source) for source, target in forward]
        low = lax.ppermute(
            lax.slice_in_dim(block, block.shape[dim] - width, None, axis=dim), axis, forward
        )
        high = lax.ppermute(lax.slice_in_dim(block, 0, width, axis=dim), axis, backward)
        block = jnp.concatenate([low, block, high], axis=dim)
    return block


def local(solutions, point_of_slot, mass_blocks, block_cols, sources):
    local_points = solutions.shape[0]
    rows_here = solutions.shape[1]
    width = solutions.shape[2] // 2
    block_size = mass_blocks.shape[2]
    span_blocks = rows_here // block_size
    total_points = local_points * lax.axis_size("quad")
    theta = 2.0 * math.pi * (point_of_slot.astype(jnp.float32) + 0.5) / total_points
    powers = jnp.arange(1, MOMENTS + 1, dtype=jnp.float32)
    angles = powers[:, None] * theta[None, :]
    cosine = (jnp.cos(angles) / total_points).astype(jnp.bfloat16)
    sine = (jnp.sin(angles) / total_points).astype(jnp.bfloat16)
    weighting = jnp.concatenate(
        [jnp.concatenate([cosine, -sine], axis=1), jnp.concatenate([sine, cosine], axis=1)], axis=0
    )
    stacked = jnp.concatenate([solutions[:, :, :width], solutions[:, :, width:]], axis=0).reshape(
        2 * local_points, rows_here * width
    )
    product = jnp.dot(weighting, stacked, preferred_element_type=jnp.float32).reshape(
        2, MOMENTS, rows_here, width
    )
    partial_value = jnp.concatenate([product[0], product[1]], axis=2)
    summed = lax.psum_scatter(
        partial_value.astype(jnp.bfloat16), "quad", scatter_dimension=0, tiled=True
    )
    widened = with_halo(summed, (("rows", 1),), rows_here)
    owned = widened.shape[0]
    panel_blocks = widened.reshape(owned, 3 * span_blocks, block_size, 2 * width)
    offset = (lax.axis_index("rows") - 1) * span_blocks
    local_cols = block_cols - offset

    def add_slot(slot_index, accum):
        columns_now = lax.dynamic_index_in_dim(local_cols, slot_index, 1, keepdims=False)
        tiles = lax.dynamic_index_in_dim(mass_blocks, slot_index, 1, keepdims=False)
        chosen = jnp.take(panel_blocks, columns_now, axis=1)
        return accum + jnp.einsum(
            "bij,mbjc->mbic", tiles, chosen, preferred_element_type=jnp.float32
        )

    start = jnp.zeros((owned, span_blocks, block_size, 2 * width), jnp.float32)
    accum = lax.fori_loop(0, mass_blocks.shape[1], add_slot, start)
    mass_applied = accum.astype(jnp.bfloat16).reshape(owned, rows_here, 2 * width)
    term = jnp.einsum("nl,mnc->mlc", sources, mass_applied, preferred_element_type=jnp.float32)
    reduced = lax.psum(term, "rows")
    return (mass_applied, reduced)


def solution(mesh):
    in_specs = (
        P("quad", ("group", "rows"), None),
        P(("group", "quad")),
        P(("group", "rows"), None, None, None),
        P(("group", "rows"), None),
        P(("group", "rows"), None),
    )
    out_specs = (P("quad", ("group", "rows"), None), P(("group", "quad"), None, None))
    return jax.shard_map(local, mesh=mesh, in_specs=in_specs, out_specs=out_specs, check_vma=False)
```

profile of v0, /device:TPU:0, one launch (start us, length us, event | category | flops | bytes accessed | tf_op | source)
XLA Modules:
  0.0 360.4 jit_solution(8767919289996625870)
XLA Ops:
  8.2 9.6 %fusion.22 = (bf16[16,1280,64]{2,1,0:T(8,128)(2,1)}, bf16[16,1280,64]{2,1,0:T(8,128)(2,1)}) fusion(bf16[16,1280,128]{2,1,0:T(8,128)(2,1)} %param.7), kind=kLoop, calls=%fused_computation.37 | loop fusion | bytes 10485760 | tf_op jit(solution)/shard_map/slice | solution.py:38
  17.8 10.4 %pad_maximum_fusion = bf16[32,1280,64]{2,1,0:T(8,128)(2,1)} fusion(bf16[16,1280,64]{2,1,0:T(8,128)(2,1)} %get-tuple-element.138, bf16[16,1280,64]{2,1,0:T(8,128)(2,1)} %get-tuple-element.137), kind=kLoop, calls=%fused_computation.14 | loop fusion | flops 2621440 | bytes 10485760 | tf_op jit(solution)/shard_map/concatenate | solution.py:38
  28.2 11.0 %reshape.29 = bf16[32,81920]{1,0:T(8,128)(2,1)} reshape(bf16[32,1280,64]{2,1,0:T(8,128)(2,1)} %pad_maximum_fusion) | data formatting | bytes 10485760 | tf_op jit(solution)/shard_map/reshape | solution.py:38
  51.6 4.3 %squeeze.21 = bf16[8,1280,64]{2,1,0:T(8,128)(2,1)} reshape(bf16[655360]{0:T(1024)(128)(2,1)} %reshape.45) | data formatting | bytes 2621440 | tf_op jit(solution)/shard_map/squeeze | solution.py:44
  55.9 4.7 %pad_maximum_fusion.2 = bf16[8,1280,128]{2,1,0:T(8,128)(2,1)} fusion(bf16[8,1280,64]{2,1,0:T(8,128)(2,1)} %squeeze.21, bf16[8,1280,64]{2,1,0:T(8,128)(2,1)S(1)} %squeeze.20), kind=kLoop, calls=%fused_computation.16 | loop fusion | flops 5242880 | bytes 5242880 | tf_op jit(solution)/shard_map/concatenate | solution.py:44
  60.6 13.0 %reduce-scatter.2.cloned.1.call-done = bf16[4,1280,128]{2,1,0:T(8,128)(2,1)} async-done(((bf16[8,1280,128]{2,1,0:T(8,128)(2,1)}), bf16[4,1280,128]{2,1,0:T(8,128)(2,1)}) %reduce-scatter.2.cloned.1.call-update) | async-done | bytes 1310736 | tf_op jit(solution)/shard_map/reduce_scatter | solution.py:45
  78.8 55.3 %collective-permute-done = bf16[4,1280,128]{2,1,0:T(8,128)(2,1)S(1)} collective-permute-done((bf16[4,1280,128]{2,1,0:T(8,128)(2,1)}, bf16[4,1280,128]{2,1,0:T(8,128)(2,1)S(1)}, u32[]{:S(2)}, u32[]{:S(2)}) %collective-permute-start) | collective-permute-done | bytes 1310752 | tf_op jit(solution)/shard_map/ppermute | solution.py:15
  137.2 139.2 %while.14 = (s32[]{:T(128)}, f32[4,10,128,128]{2,3,0,1:T(8,128)}, s32[10,20]{0,1:T(8,128)S(1)}, bf16[4,30,128,128]{3,2,1,0:T(8,128)(2,1)}, bf16[10,20,128,128]{3,2,1,0:T(8,128)(2,1)}, /*index=5*/s32[]{:T(128)}, s32[]{:T(128)}) while((s32[]{:T(128)}, f32[4,10,128,128]{2,3,0,1:T(8,128)}, s32[10,20]{0,1:T(8,128)S(1)}, ...), condition=%wide.region_2.3_spmd.clone, body=%wide.region_1.2_spmd.clone.sunk | while | flops 169739328 | bytes 9507599 | solution.py:63
  146.3 4.1 %bitcast_add_fusion.2 = f32[4,10,128,128]{2,3,0,1:T(8,128)} fusion(f32[4,10,128,128]{2,3,0,1:T(8,128)} %get-tuple-element.186, bf16[10,4,128,128]{3,2,1,0:T(8,128)(2,1)S(1)} %gather_fusion, pred[10]{0:T(512)(128)(4,1)S(1)} %get-tuple-element.177, pred[]{:T(512)S(6)} %compare.3, bf16[10,20,128,128]{3,2,1,0:T(8,128)(2,1)} %get-tuple-element.196, ...), kind=kOutput, calls=%fused_computation.1.clone.1 | convolution fusion | flops 169738240 | bytes 6881803 | tf_op jit(solution)/shard_map/while/body/eval_jaxpr/bij,mbjc->mbic/dot_general | solution.py:58
  153.3 4.1 %bitcast_add_fusion.2 = f32[4,10,128,128]{2,3,0,1:T(8,128)} fusion(f32[4,10,128,128]{2,3,0,1:T(8,128)} %get-tuple-element.186, bf16[10,4,128,128]{3,2,1,0:T(8,128)(2,1)S(1)} %gather_fusion, pred[10]{0:T(512)(128)(4,1)S(1)} %get-tuple-element.177, pred[]{:T(512)S(6)} %compare.3, bf16[10,20,128,128]{3,2,1,0:T(8,128)(2,1)} %get-tuple-element.196, ...), kind=kOutput, calls=%fused_computation.1.clone.1 | convolution fusion | flops 169738240 | bytes 6881803 | tf_op jit(solution)/shard_map/while/body/eval_jaxpr/bij,mbjc->mbic/dot_general | solution.py:58
  160.3 4.1 %bitcast_add_fusion.2 = f32[4,10,128,128]{2,3,0,1:T(8,128)} fusion(f32[4,10,128,128]{2,3,0,1:T(8,128)} %get-tuple-element.186, bf16[10,4,128,128]{3,2,1,0:T(8,128)(2,1)S(1)} %gather_fusion, pred[10]{0:T(512)(128)(4,1)S(1)} %get-tuple-element.177, pred[]{:T(512)S(6)} %compare.3, bf16[10,20,128,128]{3,2,1,0:T(8,128)(2,1)} %get-tuple-element.196, ...), kind=kOutput, calls=%fused_computation.1.clone.1 | convolution fusion | flops 169738240 | bytes 6881803 | tf_op jit(solution)/shard_map/while/body/eval_jaxpr/bij,mbjc->mbic/dot_general | solution.py:58
  167.3 4.1 %bitcast_add_fusion.2 = f32[4,10,128,128]{2,3,0,1:T(8,128)} fusion(f32[4,10,128,128]{2,3,0,1:T(8,128)} %get-tuple-element.186, bf16[10,4,128,128]{3,2,1,0:T(8,128)(2,1)S(1)} %gather_fusion, pred[10]{0:T(512)(128)(4,1)S(1)} %get-tuple-element.177, pred[]{:T(512)S(6)} %compare.3, bf16[10,20,128,128]{3,2,1,0:T(8,128)(2,1)} %get-tuple-element.196, ...), kind=kOutput, calls=%fused_computation.1.clone.1 | convolution fusion | flops 169738240 | bytes 6881803 | tf_op jit(solution)/shard_map/while/body/eval_jaxpr/bij,mbjc->mbic/dot_general | solution.py:58
  174.3 4.1 %bitcast_add_fusion.2 = f32[4,10,128,128]{2,3,0,1:T(8,128)} fusion(f32[4,10,128,128]{2,3,0,1:T(8,128)} %get-tuple-element.186, bf16[10,4,128,128]{3,2,1,0:T(8,128)(2,1)S(1)} %gather_fusion, pred[10]{0:T(512)(128)(4,1)S(1)} %get-tuple-element.177, pred[]{:T(512)S(6)} %compare.3, bf16[10,20,128,128]{3,2,1,0:T(8,128)(2,1)} %get-tuple-element.196, ...), kind=kOutput, calls=%fused_computation.1.clone.1 | convolution fusion | flops 169738240 | bytes 6881803 | tf_op jit(solution)/shard_map/while/body/eval_jaxpr/bij,mbjc->mbic/dot_general | solution.py:58
  181.3 4.1 %bitcast_add_fusion.2 = f32[4,10,128,128]{2,3,0,1:T(8,128)} fusion(f32[4,10,128,128]{2,3,0,1:T(8,128)} %get-tuple-element.186, bf16[10,4,128,128]{3,2,1,0:T(8,128)(2,1)S(1)} %gather_fusion, pred[10]{0:T(512)(128)(4,1)S(1)} %get-tuple-element.177, pred[]{:T(512)S(6)} %compare.3, bf16[10,20,128,128]{3,2,1,0:T(8,128)(2,1)} %get-tuple-element.196, ...), kind=kOutput, calls=%fused_computation.1.clone.1 | convolution fusion | flops 169738240 | bytes 6881803 | tf_op jit(solution)/shard_map/while/body/eval_jaxpr/bij,mbjc->mbic/dot_general | solution.py:58
  202.3 4.1 %bitcast_add_fusion.2 = f32[4,10,128,128]{2,3,0,1:T(8,128)} fusion(f32[4,10,128,128]{2,3,0,1:T(8,128)} %get-tuple-element.186, bf16[10,4,128,128]{3,2,1,0:T(8,128)(2,1)S(1)} %gather_fusion, pred[10]{0:T(512)(128)(4,1)S(1)} %get-tuple-element.177, pred[]{:T(512)S(6)} %compare.3, bf16[10,20,128,128]{3,2,1,0:T(8,128)(2,1)} %get-tuple-element.196, ...), kind=kOutput, calls=%fused_computation.1.clone.1 | convolution fusion | flops 169738240 | bytes 6881803 | tf_op jit(solution)/shard_map/while/body/eval_jaxpr/bij,mbjc->mbic/dot_general | solution.py:58
  209.3 4.1 %bitcast_add_fusion.2 = f32[4,10,128,128]{2,3,0,1:T(8,128)} fusion(f32[4,10,128,128]{2,3,0,1:T(8,128)} %get-tuple-element.186, bf16[10,4,128,128]{3,2,1,0:T(8,128)(2,1)S(1)} %gather_fusion, pred[10]{0:T(512)(128)(4,1)S(1)} %get-tuple-element.177, pred[]{:T(512)S(6)} %compare.3, bf16[10,20,128,128]{3,2,1,0:T(8,128)(2,1)} %get-tuple-element.196, ...), kind=kOutput, calls=%fused_computation.1.clone.1 | convolution fusion | flops 169738240 | bytes 6881803 | tf_op jit(solution)/shard_map/while/body/eval_jaxpr/bij,mbjc->mbic/dot_general | solution.py:58
  216.3 4.1 %bitcast_add_fusion.2 = f32[4,10,128,128]{2,3,0,1:T(8,128)} fusion(f32[4,10,128,128]{2,3,0,1:T(8,128)} %get-tuple-element.186, bf16[10,4,128,128]{3,2,1,0:T(8,128)(2,1)S(1)} %gather_fusion, pred[10]{0:T(512)(128)(4,1)S(1)} %get-tuple-element.177, pred[]{:T(512)S(6)} %compare.3, bf16[10,20,128,128]{3,2,1,0:T(8,128)(2,1)} %get-tuple-element.196, ...), kind=kOutput, calls=%fused_computation.1.clone.1 | convolution fusion | flops 169738240 | bytes 6881803 | tf_op jit(solution)/shard_map/while/body/eval_jaxpr/bij,mbjc->mbic/dot_general | solution.py:58
  223.4 4.1 %bitcast_add_fusion.2 = f32[4,10,128,128]{2,3,0,1:T(8,128)} fusion(f32[4,10,128,128]{2,3,0,1:T(8,128)} %get-tuple-element.186, bf16[10,4,128,128]{3,2,1,0:T(8,128)(2,1)S(1)} %gather_fusion, pred[10]{0:T(512)(128)(4,1)S(1)} %get-tuple-element.177, pred[]{:T(512)S(6)} %compare.3, bf16[10,20,128,128]{3,2,1,0:T(8,128)(2,1)} %get-tuple-element.196, ...), kind=kOutput, calls=%fused_computation.1.clone.1 | convolution fusion | flops 169738240 | bytes 6881803 | tf_op jit(solution)/shard_map/while/body/eval_jaxpr/bij,mbjc->mbic/dot_general | solution.py:58
  230.4 4.1 %bitcast_add_fusion.2 = f32[4,10,128,128]{2,3,0,1:T(8,128)} fusion(f32[4,10,128,128]{2,3,0,1:T(8,128)} %get-tuple-element.186, bf16[10,4,128,128]{3,2,1,0:T(8,128)(2,1)S(1)} %gather_fusion, pred[10]{0:T(512)(128)(4,1)S(1)} %get-tuple-element.177, pred[]{:T(512)S(6)} %compare.3, bf16[10,20,128,128]{3,2,1,0:T(8,128)(2,1)} %get-tuple-element.196, ...), kind=kOutput, calls=%fused_computation.1.clone.1 | convolution fusion | flops 169738240 | bytes 6881803 | tf_op jit(solution)/shard_map/while/body/eval_jaxpr/bij,mbjc->mbic/dot_general | solution.py:58
  237.4 4.1 %bitcast_add_fusion.2 = f32[4,10,128,128]{2,3,0,1:T(8,128)} fusion(f32[4,10,128,128]{2,3,0,1:T(8,128)} %get-tuple-element.186, bf16[10,4,128,128]{3,2,1,0:T(8,128)(2,1)S(1)} %gather_fusion, pred[10]{0:T(512)(128)(4,1)S(1)} %get-tuple-element.177, pred[]{:T(512)S(6)} %compare.3, bf16[10,20,128,128]{3,2,1,0:T(8,128)(2,1)} %get-tuple-element.196, ...), kind=kOutput, calls=%fused_computation.1.clone.1 | convolution fusion | flops 169738240 | bytes 6881803 | tf_op jit(solution)/shard_map/while/body/eval_jaxpr/bij,mbjc->mbic/dot_general | solution.py:58
  244.4 4.1 %bitcast_add_fusion.2 = f32[4,10,128,128]{2,3,0,1:T(8,128)} fusion(f32[4,10,128,128]{2,3,0,1:T(8,128)} %get-tuple-element.186, bf16[10,4,128,128]{3,2,1,0:T(8,128)(2,1)S(1)} %gather_fusion, pred[10]{0:T(512)(128)(4,1)S(1)} %get-tuple-element.177, pred[]{:T(512)S(6)} %compare.3, bf16[10,20,128,128]{3,2,1,0:T(8,128)(2,1)} %get-tuple-element.196, ...), kind=kOutput, calls=%fused_computation.1.clone.1 | convolution fusion | flops 169738240 | bytes 6881803 | tf_op jit(solution)/shard_map/while/body/eval_jaxpr/bij,mbjc->mbic/dot_general | solution.py:58
  251.4 4.1 %bitcast_add_fusion.2 = f32[4,10,128,128]{2,3,0,1:T(8,128)} fusion(f32[4,10,128,128]{2,3,0,1:T(8,128)} %get-tuple-element.186, bf16[10,4,128,128]{3,2,1,0:T(8,128)(2,1)S(1)} %gather_fusion, pred[10]{0:T(512)(128)(4,1)S(1)} %get-tuple-element.177, pred[]{:T(512)S(6)} %compare.3, bf16[10,20,128,128]{3,2,1,0:T(8,128)(2,1)} %get-tuple-element.196, ...), kind=kOutput, calls=%fused_computation.1.clone.1 | convolution fusion | flops 169738240 | bytes 6881803 | tf_op jit(solution)/shard_map/while/body/eval_jaxpr/bij,mbjc->mbic/dot_general | solution.py:58
  265.4 4.1 %bitcast_add_fusion.2 = f32[4,10,128,128]{2,3,0,1:T(8,128)} fusion(f32[4,10,128,128]{2,3,0,1:T(8,128)} %get-tuple-element.186, bf16[10,4,128,128]{3,2,1,0:T(8,128)(2,1)S(1)} %gather_fusion, pred[10]{0:T(512)(128)(4,1)S(1)} %get-tuple-element.177, pred[]{:T(512)S(6)} %compare.3, bf16[10,20,128,128]{3,2,1,0:T(8,128)(2,1)} %get-tuple-element.196, ...), kind=kOutput, calls=%fused_computation.1.clone.1 | convolution fusion | flops 169738240 | bytes 6881803 | tf_op jit(solution)/shard_map/while/body/eval_jaxpr/bij,mbjc->mbic/dot_general | solution.py:58
  280.3 71.7 %all-reduce.2.cloned.1.call-done = f32[4,64,128]{2,1,0:T(8,128)} async-done(((f32[4,64,128]{2,1,0:T(8,128)}), f32[4,64,128]{2,1,0:T(8,128)}) %all-reduce.2.cloned.1.call-update) | async-done | bytes 131088 | tf_op jit(solution)/shard_map/psum | solution.py:66
  (95 shorter events, 105.0 us)
Async XLA Ops:
  7.2 272.0 %copy-start = (bf16[1280,64]{0,1:T(8,128)(2,1)S(1)}, bf16[1280,64]{0,1:T(8,128)(2,1)}, u32[]{:S(2)}) copy-start(bf16[1280,64]{0,1:T(8,128)(2,1)} %param.11) | copy-start | bytes 491524
  7.2 66.4 %reduce-scatter.2.cloned.1.call-start = ((), (), s32[]{:S(2)}) async-start(), calls=%async_computation.1 | async-start | bytes 3932160 | tf_op jit(solution)/shard_map/reduce_scatter | solution.py:45
  60.6 18.2 %copy-start.2 = (s32[10,20]{1,0:T(8,128)S(1)}, s32[10,20]{1,0:T(8,128)}, u32[]{:S(2)}) copy-start(s32[10,20]{1,0:T(8,128)} %param.10) | copy-start | bytes 2404
  60.6 291.4 %all-reduce.2.cloned.1.call-start = ((), (), s32[]{:S(2)}) async-start(), calls=%async_computation.2 | async-start | bytes 262144 | tf_op jit(solution)/shard_map/psum | solution.py:66
  73.6 60.5 %collective-permute-start = (bf16[4,1280,128]{2,1,0:T(8,128)(2,1)}, bf16[4,1280,128]{2,1,0:T(8,128)(2,1)S(1)}, u32[]{:S(2)}, u32[]{:S(2)}) collective-permute-start(bf16[4,1280,128]{2,1,0:T(8,128)(2,1)} %reduce-scatter.2.cloned.1.call-done), channel_id=1, source_target_pairs={{0,1},{1,2},{2,3},{3,4},{4,5},{5,6},{6,7},{8,9},{9,10},{10,11},{11... | collective-permute-start | bytes 3932168 | tf_op jit(solution)/shard_map/ppermute | solution.py:15
  77.4 56.7 %collective-permute-start.1 = (bf16[4,1280,128]{2,1,0:T(8,128)(2,1)}, bf16[4,1280,128]{2,1,0:T(8,128)(2,1)S(1)}, u32[]{:S(2)}, u32[]{:S(2)}) collective-permute-start(bf16[4,1280,128]{2,1,0:T(8,128)(2,1)} %reduce-scatter.2.cloned.1.call-done), channel_id=1, source_target_pairs={{1,0},{2,1},{3,2},{4,3},{5,4},{6,5},{7,6},{9,8},{10,9},{11,10},{12... | collective-permute-start | bytes 3932168 | tf_op jit(solution)/shard_map/ppermute | solution.py:18
  279.2 74.4 %copy-start.1 = (bf16[4,10,128,128]{3,2,1,0:T(8,128)(2,1)}, bf16[4,10,128,128]{3,2,1,0:T(8,128)(2,1)S(1)}, u32[]{:S(2)}) copy-start(bf16[4,10,128,128]{3,2,1,0:T(8,128)(2,1)S(1)} %copy.14) | copy-start | bytes 3932164
Sparse Core Ops, SparseCore 0:
  60.7 12.8 reduce-scatter.1
  280.4 71.5 all-reduce.1
where the time goes:
time: 363 us; the launch traced here: 360 us
  waiting for transfers between devices  140 us (39%)
  local copies, waits for them, and re-layouts  94.6 us (26%)
  matrix products  84.7 us (23%)
  other arithmetic  21.4 us (6%)
  between operations  14.1 us (4%)
  starting transfers between devices  5.14 us (1%)
    dot_general x20, matrix products, add_slot(): jnp.einsum('bij,mbjc->mbic', tiles, chosen, preferred_element_type=jnp.fl...  80.2 us
    psum x1, waiting for transfers between devices, local(): reduced = lax.psum(term, 'rows')  71.7 us
    gather x20, local copies, waits for them, and re-layouts, add_slot(): chosen = jnp.take(panel_blocks, columns_now, axis=1)  58.2 us
    ppermute x1, waiting for transfers between devices, with_halo(): lax.ppermute(lax.slice_in_dim(block, block.shape[dim] - width, None, axis...  55.3 us
    reduce_scatter x1, waiting for transfers between devices, local(): lax.psum_scatter(partial_value.astype(jnp.bfloat16), 'quad', scatter_dime...  13 us
    reshape x1, local copies, waits for them, and re-layouts, local(): jnp.concatenate([solutions[:, :, :width], solutions[:, :, width:]], axis=0)  11 us
    concatenate x1, other arithmetic, local(): jnp.concatenate([solutions[:, :, :width], solutions[:, :, width:]], axis=0)  10.4 us
    slice x1, local copies, waits for them, and re-layouts, local(): solutions[:, :, :width]  9.61 us
  transfers between devices with their start and end apart: 4, of which 3 were waited for; matrix products, arithmetic and copies ran while one was open for 0% of the time, Pallas kernels for 0%

commit v1 on v0

--- a/solution.py
+++ b/solution.py
@@ -63,7 +63,7 @@
     accum = lax.fori_loop(0, mass_blocks.shape[1], add_slot, start)
     mass_applied = accum.astype(jnp.bfloat16).reshape(owned, rows_here, 2 * width)
     term = jnp.einsum("nl,mnc->mlc", sources, mass_applied, preferred_element_type=jnp.float32)
-    reduced = lax.psum(term, "rows")
+    reduced = jnp.sum(lax.all_gather(term, "rows"), axis=0)
     return (mass_applied, reduced)
 
 

time: 363 us -> 333 us (0.917)
  waiting for transfers between devices: 140 us -> 110 us
    psum x1 -> x0, waiting for transfers between devices: 71.7 us -> none  [local(): reduced = lax.psum(term, 'rows')]
    all_gather x0 -> x1, waiting for transfers between devices: none -> 42.1 us  [local(): reduced = jnp.sum(lax.all_gather(term, 'rows'), axis=0)]
where the time goes in v1:
time: 333 us; the launch traced here: 331 us
  waiting for transfers between devices  110 us (33%)
  local copies, waits for them, and re-layouts  93 us (28%)
  matrix products  84.7 us (25%)
  other arithmetic  23.3 us (7%)
  between operations  14.1 us (4%)
  starting transfers between devices  5.14 us (2%)
    dot_general x20, matrix products, add_slot(): jnp.einsum('bij,mbjc->mbic', tiles, chosen, preferred_element_type=jnp.fl...  80.2 us
    gather x20, local copies, waits for them, and re-layouts, add_slot(): chosen = jnp.take(panel_blocks, columns_now, axis=1)  58.2 us
    ppermute x1, waiting for transfers between devices, with_halo(): lax.ppermute(lax.slice_in_dim(block, block.shape[dim] - width, None, axis...  55.3 us
    all_gather x1, waiting for transfers between devices, local(): reduced = jnp.sum(lax.all_gather(term, 'rows'), axis=0)  42.1 us
    reduce_scatter x1, waiting for transfers between devices, local(): lax.psum_scatter(partial_value.astype(jnp.bfloat16), 'quad', scatter_dime...  13 us
    reshape x1, local copies, waits for them, and re-layouts, local(): jnp.concatenate([solutions[:, :, :width], solutions[:, :, width:]], axis=0)  11 us
    concatenate x1, other arithmetic, local(): jnp.concatenate([solutions[:, :, :width], solutions[:, :, width:]], axis=0)  10.4 us
    slice x1, local copies, waits for them, and re-layouts, local(): solutions[:, :, :width]  9.61 us
  transfers between devices with their start and end apart: 4, of which 3 were waited for; matrix products, arithmetic and copies ran while one was open for 0% of the time, Pallas kernels for 0%

profile of v1, /device:TPU:0, one launch (start us, length us, event | category | flops | bytes accessed | tf_op | source)
XLA Modules:
  0.0 331.2 jit_solution(13735670911149692483)
XLA Ops:
  8.2 9.6 %fusion.22 = (bf16[16,1280,64]{2,1,0:T(8,128)(2,1)}, bf16[16,1280,64]{2,1,0:T(8,128)(2,1)}) fusion(bf16[16,1280,128]{2,1,0:T(8,128)(2,1)} %param.7), kind=kLoop, calls=%fused_computation.37 | loop fusion | bytes 10485760 | tf_op jit(solution)/shard_map/slice | solution.py:38
  17.8 10.4 %pad_maximum_fusion = bf16[32,1280,64]{2,1,0:T(8,128)(2,1)} fusion(bf16[16,1280,64]{2,1,0:T(8,128)(2,1)} %get-tuple-element.143, bf16[16,1280,64]{2,1,0:T(8,128)(2,1)} %get-tuple-element.142), kind=kLoop, calls=%fused_computation.14 | loop fusion | flops 2621440 | bytes 10485760 | tf_op jit(solution)/shard_map/concatenate | solution.py:38
  28.2 11.0 %reshape.29 = bf16[32,81920]{1,0:T(8,128)(2,1)} reshape(bf16[32,1280,64]{2,1,0:T(8,128)(2,1)} %pad_maximum_fusion) | data formatting | bytes 10485760 | tf_op jit(solution)/shard_map/reshape | solution.py:38
  51.6 4.3 %squeeze.21 = bf16[8,1280,64]{2,1,0:T(8,128)(2,1)} reshape(bf16[655360]{0:T(1024)(128)(2,1)} %reshape.46) | data formatting | bytes 2621440 | tf_op jit(solution)/shard_map/squeeze | solution.py:44
  55.9 4.7 %pad_maximum_fusion.2 = bf16[8,1280,128]{2,1,0:T(8,128)(2,1)} fusion(bf16[8,1280,64]{2,1,0:T(8,128)(2,1)} %squeeze.21, bf16[8,1280,64]{2,1,0:T(8,128)(2,1)S(1)} %squeeze.20), kind=kLoop, calls=%fused_computation.16 | loop fusion | flops 5242880 | bytes 5242880 | tf_op jit(solution)/shard_map/concatenate | solution.py:44
  60.6 13.0 %reduce-scatter.2.cloned.1.call-done = bf16[4,1280,128]{2,1,0:T(8,128)(2,1)} async-done(((bf16[8,1280,128]{2,1,0:T(8,128)(2,1)}), bf16[4,1280,128]{2,1,0:T(8,128)(2,1)}) %reduce-scatter.2.cloned.1.call-update) | async-done | bytes 1310736 | tf_op jit(solution)/shard_map/reduce_scatter | solution.py:45
  78.8 55.3 %collective-permute-done = bf16[4,1280,128]{2,1,0:T(8,128)(2,1)S(1)} collective-permute-done((bf16[4,1280,128]{2,1,0:T(8,128)(2,1)}, bf16[4,1280,128]{2,1,0:T(8,128)(2,1)S(1)}, u32[]{:S(2)}, u32[]{:S(2)}) %collective-permute-start) | collective-permute-done | bytes 1310752 | tf_op jit(solution)/shard_map/ppermute | solution.py:15
  137.2 139.2 %while.14 = (s32[]{:T(128)}, f32[4,10,128,128]{2,3,0,1:T(8,128)}, s32[10,20]{0,1:T(8,128)S(1)}, bf16[4,30,128,128]{3,2,1,0:T(8,128)(2,1)}, bf16[10,20,128,128]{3,2,1,0:T(8,128)(2,1)}, /*index=5*/s32[]{:T(128)}, s32[]{:T(128)}) while((s32[]{:T(128)}, f32[4,10,128,128]{2,3,0,1:T(8,128)}, s32[10,20]{0,1:T(8,128)S(1)}, ...), condition=%wide.region_2.3_spmd.clone, body=%wide.region_1.2_spmd.clone.sunk | while | flops 169739328 | bytes 9507599 | solution.py:63
  146.3 4.1 %bitcast_add_fusion.2 = f32[4,10,128,128]{2,3,0,1:T(8,128)} fusion(f32[4,10,128,128]{2,3,0,1:T(8,128)} %get-tuple-element.191, bf16[10,4,128,128]{3,2,1,0:T(8,128)(2,1)S(1)} %gather_fusion, pred[10]{0:T(512)(128)(4,1)S(1)} %get-tuple-element.182, pred[]{:T(512)S(6)} %compare.3, bf16[10,20,128,128]{3,2,1,0:T(8,128)(2,1)} %get-tuple-element.201, ...), kind=kOutput, calls=%fused_computation.1.clone.1 | convolution fusion | flops 169738240 | bytes 6881803 | tf_op jit(solution)/shard_map/while/body/eval_jaxpr/bij,mbjc->mbic/dot_general | solution.py:58
  153.3 4.1 %bitcast_add_fusion.2 = f32[4,10,128,128]{2,3,0,1:T(8,128)} fusion(f32[4,10,128,128]{2,3,0,1:T(8,128)} %get-tuple-element.191, bf16[10,4,128,128]{3,2,1,0:T(8,128)(2,1)S(1)} %gather_fusion, pred[10]{0:T(512)(128)(4,1)S(1)} %get-tuple-element.182, pred[]{:T(512)S(6)} %compare.3, bf16[10,20,128,128]{3,2,1,0:T(8,128)(2,1)} %get-tuple-element.201, ...), kind=kOutput, calls=%fused_computation.1.clone.1 | convolution fusion | flops 169738240 | bytes 6881803 | tf_op jit(solution)/shard_map/while/body/eval_jaxpr/bij,mbjc->mbic/dot_general | solution.py:58
  160.3 4.1 %bitcast_add_fusion.2 = f32[4,10,128,128]{2,3,0,1:T(8,128)} fusion(f32[4,10,128,128]{2,3,0,1:T(8,128)} %get-tuple-element.191, bf16[10,4,128,128]{3,2,1,0:T(8,128)(2,1)S(1)} %gather_fusion, pred[10]{0:T(512)(128)(4,1)S(1)} %get-tuple-element.182, pred[]{:T(512)S(6)} %compare.3, bf16[10,20,128,128]{3,2,1,0:T(8,128)(2,1)} %get-tuple-element.201, ...), kind=kOutput, calls=%fused_computation.1.clone.1 | convolution fusion | flops 169738240 | bytes 6881803 | tf_op jit(solution)/shard_map/while/body/eval_jaxpr/bij,mbjc->mbic/dot_general | solution.py:58
  167.3 4.1 %bitcast_add_fusion.2 = f32[4,10,128,128]{2,3,0,1:T(8,128)} fusion(f32[4,10,128,128]{2,3,0,1:T(8,128)} %get-tuple-element.191, bf16[10,4,128,128]{3,2,1,0:T(8,128)(2,1)S(1)} %gather_fusion, pred[10]{0:T(512)(128)(4,1)S(1)} %get-tuple-element.182, pred[]{:T(512)S(6)} %compare.3, bf16[10,20,128,128]{3,2,1,0:T(8,128)(2,1)} %get-tuple-element.201, ...), kind=kOutput, calls=%fused_computation.1.clone.1 | convolution fusion | flops 169738240 | bytes 6881803 | tf_op jit(solution)/shard_map/while/body/eval_jaxpr/bij,mbjc->mbic/dot_general | solution.py:58
  174.3 4.1 %bitcast_add_fusion.2 = f32[4,10,128,128]{2,3,0,1:T(8,128)} fusion(f32[4,10,128,128]{2,3,0,1:T(8,128)} %get-tuple-element.191, bf16[10,4,128,128]{3,2,1,0:T(8,128)(2,1)S(1)} %gather_fusion, pred[10]{0:T(512)(128)(4,1)S(1)} %get-tuple-element.182, pred[]{:T(512)S(6)} %compare.3, bf16[10,20,128,128]{3,2,1,0:T(8,128)(2,1)} %get-tuple-element.201, ...), kind=kOutput, calls=%fused_computation.1.clone.1 | convolution fusion | flops 169738240 | bytes 6881803 | tf_op jit(solution)/shard_map/while/body/eval_jaxpr/bij,mbjc->mbic/dot_general | solution.py:58
  181.3 4.1 %bitcast_add_fusion.2 = f32[4,10,128,128]{2,3,0,1:T(8,128)} fusion(f32[4,10,128,128]{2,3,0,1:T(8,128)} %get-tuple-element.191, bf16[10,4,128,128]{3,2,1,0:T(8,128)(2,1)S(1)} %gather_fusion, pred[10]{0:T(512)(128)(4,1)S(1)} %get-tuple-element.182, pred[]{:T(512)S(6)} %compare.3, bf16[10,20,128,128]{3,2,1,0:T(8,128)(2,1)} %get-tuple-element.201, ...), kind=kOutput, calls=%fused_computation.1.clone.1 | convolution fusion | flops 169738240 | bytes 6881803 | tf_op jit(solution)/shard_map/while/body/eval_jaxpr/bij,mbjc->mbic/dot_general | solution.py:58
  202.3 4.1 %bitcast_add_fusion.2 = f32[4,10,128,128]{2,3,0,1:T(8,128)} fusion(f32[4,10,128,128]{2,3,0,1:T(8,128)} %get-tuple-element.191, bf16[10,4,128,128]{3,2,1,0:T(8,128)(2,1)S(1)} %gather_fusion, pred[10]{0:T(512)(128)(4,1)S(1)} %get-tuple-element.182, pred[]{:T(512)S(6)} %compare.3, bf16[10,20,128,128]{3,2,1,0:T(8,128)(2,1)} %get-tuple-element.201, ...), kind=kOutput, calls=%fused_computation.1.clone.1 | convolution fusion | flops 169738240 | bytes 6881803 | tf_op jit(solution)/shard_map/while/body/eval_jaxpr/bij,mbjc->mbic/dot_general | solution.py:58
  209.3 4.1 %bitcast_add_fusion.2 = f32[4,10,128,128]{2,3,0,1:T(8,128)} fusion(f32[4,10,128,128]{2,3,0,1:T(8,128)} %get-tuple-element.191, bf16[10,4,128,128]{3,2,1,0:T(8,128)(2,1)S(1)} %gather_fusion, pred[10]{0:T(512)(128)(4,1)S(1)} %get-tuple-element.182, pred[]{:T(512)S(6)} %compare.3, bf16[10,20,128,128]{3,2,1,0:T(8,128)(2,1)} %get-tuple-element.201, ...), kind=kOutput, calls=%fused_computation.1.clone.1 | convolution fusion | flops 169738240 | bytes 6881803 | tf_op jit(solution)/shard_map/while/body/eval_jaxpr/bij,mbjc->mbic/dot_general | solution.py:58
  216.3 4.1 %bitcast_add_fusion.2 = f32[4,10,128,128]{2,3,0,1:T(8,128)} fusion(f32[4,10,128,128]{2,3,0,1:T(8,128)} %get-tuple-element.191, bf16[10,4,128,128]{3,2,1,0:T(8,128)(2,1)S(1)} %gather_fusion, pred[10]{0:T(512)(128)(4,1)S(1)} %get-tuple-element.182, pred[]{:T(512)S(6)} %compare.3, bf16[10,20,128,128]{3,2,1,0:T(8,128)(2,1)} %get-tuple-element.201, ...), kind=kOutput, calls=%fused_computation.1.clone.1 | convolution fusion | flops 169738240 | bytes 6881803 | tf_op jit(solution)/shard_map/while/body/eval_jaxpr/bij,mbjc->mbic/dot_general | solution.py:58
  223.4 4.1 %bitcast_add_fusion.2 = f32[4,10,128,128]{2,3,0,1:T(8,128)} fusion(f32[4,10,128,128]{2,3,0,1:T(8,128)} %get-tuple-element.191, bf16[10,4,128,128]{3,2,1,0:T(8,128)(2,1)S(1)} %gather_fusion, pred[10]{0:T(512)(128)(4,1)S(1)} %get-tuple-element.182, pred[]{:T(512)S(6)} %compare.3, bf16[10,20,128,128]{3,2,1,0:T(8,128)(2,1)} %get-tuple-element.201, ...), kind=kOutput, calls=%fused_computation.1.clone.1 | convolution fusion | flops 169738240 | bytes 6881803 | tf_op jit(solution)/shard_map/while/body/eval_jaxpr/bij,mbjc->mbic/dot_general | solution.py:58
  230.4 4.1 %bitcast_add_fusion.2 = f32[4,10,128,128]{2,3,0,1:T(8,128)} fusion(f32[4,10,128,128]{2,3,0,1:T(8,128)} %get-tuple-element.191, bf16[10,4,128,128]{3,2,1,0:T(8,128)(2,1)S(1)} %gather_fusion, pred[10]{0:T(512)(128)(4,1)S(1)} %get-tuple-element.182, pred[]{:T(512)S(6)} %compare.3, bf16[10,20,128,128]{3,2,1,0:T(8,128)(2,1)} %get-tuple-element.201, ...), kind=kOutput, calls=%fused_computation.1.clone.1 | convolution fusion | flops 169738240 | bytes 6881803 | tf_op jit(solution)/shard_map/while/body/eval_jaxpr/bij,mbjc->mbic/dot_general | solution.py:58
  237.4 4.1 %bitcast_add_fusion.2 = f32[4,10,128,128]{2,3,0,1:T(8,128)} fusion(f32[4,10,128,128]{2,3,0,1:T(8,128)} %get-tuple-element.191, bf16[10,4,128,128]{3,2,1,0:T(8,128)(2,1)S(1)} %gather_fusion, pred[10]{0:T(512)(128)(4,1)S(1)} %get-tuple-element.182, pred[]{:T(512)S(6)} %compare.3, bf16[10,20,128,128]{3,2,1,0:T(8,128)(2,1)} %get-tuple-element.201, ...), kind=kOutput, calls=%fused_computation.1.clone.1 | convolution fusion | flops 169738240 | bytes 6881803 | tf_op jit(solution)/shard_map/while/body/eval_jaxpr/bij,mbjc->mbic/dot_general | solution.py:58
  244.4 4.1 %bitcast_add_fusion.2 = f32[4,10,128,128]{2,3,0,1:T(8,128)} fusion(f32[4,10,128,128]{2,3,0,1:T(8,128)} %get-tuple-element.191, bf16[10,4,128,128]{3,2,1,0:T(8,128)(2,1)S(1)} %gather_fusion, pred[10]{0:T(512)(128)(4,1)S(1)} %get-tuple-element.182, pred[]{:T(512)S(6)} %compare.3, bf16[10,20,128,128]{3,2,1,0:T(8,128)(2,1)} %get-tuple-element.201, ...), kind=kOutput, calls=%fused_computation.1.clone.1 | convolution fusion | flops 169738240 | bytes 6881803 | tf_op jit(solution)/shard_map/while/body/eval_jaxpr/bij,mbjc->mbic/dot_general | solution.py:58
  251.4 4.1 %bitcast_add_fusion.2 = f32[4,10,128,128]{2,3,0,1:T(8,128)} fusion(f32[4,10,128,128]{2,3,0,1:T(8,128)} %get-tuple-element.191, bf16[10,4,128,128]{3,2,1,0:T(8,128)(2,1)S(1)} %gather_fusion, pred[10]{0:T(512)(128)(4,1)S(1)} %get-tuple-element.182, pred[]{:T(512)S(6)} %compare.3, bf16[10,20,128,128]{3,2,1,0:T(8,128)(2,1)} %get-tuple-element.201, ...), kind=kOutput, calls=%fused_computation.1.clone.1 | convolution fusion | flops 169738240 | bytes 6881803 | tf_op jit(solution)/shard_map/while/body/eval_jaxpr/bij,mbjc->mbic/dot_general | solution.py:58
  265.4 4.1 %bitcast_add_fusion.2 = f32[4,10,128,128]{2,3,0,1:T(8,128)} fusion(f32[4,10,128,128]{2,3,0,1:T(8,128)} %get-tuple-element.191, bf16[10,4,128,128]{3,2,1,0:T(8,128)(2,1)S(1)} %gather_fusion, pred[10]{0:T(512)(128)(4,1)S(1)} %get-tuple-element.182, pred[]{:T(512)S(6)} %compare.3, bf16[10,20,128,128]{3,2,1,0:T(8,128)(2,1)} %get-tuple-element.201, ...), kind=kOutput, calls=%fused_computation.1.clone.1 | convolution fusion | flops 169738240 | bytes 6881803 | tf_op jit(solution)/shard_map/while/body/eval_jaxpr/bij,mbjc->mbic/dot_general | solution.py:58
  280.3 42.1 %all-gather.3.cloned.1.call-done = f32[32,64,128]{2,1,0:T(8,128)} async-done(((f32[4,64,128]{2,1,0:T(8,128)}), f32[32,64,128]{2,1,0:T(8,128)}) %all-gather.3.cloned.1.call-update) | async-done | bytes 1048592 | tf_op jit(solution)/shard_map/all_gather | solution.py:66
  (95 shorter events, 105.3 us)
Async XLA Ops:
  7.2 272.0 %copy-start = (bf16[1280,64]{0,1:T(8,128)(2,1)S(1)}, bf16[1280,64]{0,1:T(8,128)(2,1)}, u32[]{:S(2)}) copy-start(bf16[1280,64]{0,1:T(8,128)(2,1)} %param.11) | copy-start | bytes 491524
  7.2 66.4 %reduce-scatter.2.cloned.1.call-start = ((), (), s32[]{:S(2)}) async-start(), calls=%async_computation.1 | async-start | bytes 3932160 | tf_op jit(solution)/shard_map/reduce_scatter | solution.py:45
  60.6 18.2 %copy-start.2 = (s32[10,20]{1,0:T(8,128)S(1)}, s32[10,20]{1,0:T(8,128)}, u32[]{:S(2)}) copy-start(s32[10,20]{1,0:T(8,128)} %param.10) | copy-start | bytes 2404
  60.6 261.9 %all-gather.3.cloned.1.call-start = ((), (), s32[]{:S(2)}) async-start(), calls=%async_computation.2 | async-start | bytes 1179648 | tf_op jit(solution)/shard_map/all_gather | solution.py:66
  73.6 60.5 %collective-permute-start = (bf16[4,1280,128]{2,1,0:T(8,128)(2,1)}, bf16[4,1280,128]{2,1,0:T(8,128)(2,1)S(1)}, u32[]{:S(2)}, u32[]{:S(2)}) collective-permute-start(bf16[4,1280,128]{2,1,0:T(8,128)(2,1)} %reduce-scatter.2.cloned.1.call-done), channel_id=1, source_target_pairs={{0,1},{1,2},{2,3},{3,4},{4,5},{5,6},{6,7},{8,9},{9,10},{10,11},{11... | collective-permute-start | bytes 3932168 | tf_op jit(solution)/shard_map/ppermute | solution.py:15
  77.4 56.7 %collective-permute-start.1 = (bf16[4,1280,128]{2,1,0:T(8,128)(2,1)}, bf16[4,1280,128]{2,1,0:T(8,128)(2,1)S(1)}, u32[]{:S(2)}, u32[]{:S(2)}) collective-permute-start(bf16[4,1280,128]{2,1,0:T(8,128)(2,1)} %reduce-scatter.2.cloned.1.call-done), channel_id=1, source_target_pairs={{1,0},{2,1},{3,2},{4,3},{5,4},{6,5},{7,6},{9,8},{10,9},{11,10},{12... | collective-permute-start | bytes 3932168 | tf_op jit(solution)/shard_map/ppermute | solution.py:18
  279.2 45.2 %copy-start.1 = (bf16[4,10,128,128]{3,2,1,0:T(8,128)(2,1)}, bf16[4,10,128,128]{3,2,1,0:T(8,128)(2,1)S(1)}, u32[]{:S(2)}) copy-start(bf16[4,10,128,128]{3,2,1,0:T(8,128)(2,1)S(1)} %copy.18) | copy-start | bytes 3932164
Sparse Core Ops, SparseCore 0:
  60.7 12.8 reduce-scatter.1
  280.4 41.9 all-gather.2
